TPU v7x, 32 devices: a whole 2x2x4 slice. The times are simulated.
32 devices in a mesh: row: 8 (over y, x, core), rep: 4 (over z).
Axes of the slice: x: 2, y: 2, z: 4, core: 2. Of those that a mesh axis runs over, the one named last changes fastest.
Arguments:
- features: bfloat16 [8192, 256], P('row'), may hold values from -6 to 6
- weight_self: bfloat16 [256, 256], replicated, may hold values from -0.375 to 0.375
- weight_neigh: bfloat16 [256, 256], replicated, may hold values from -0.375 to 0.375
- degrees: int32 [8192], P('row'), may hold values from 1 to 47
- tile_values: bfloat16 [8, 8, 48, 128, 128], P('row', 'rep'), may hold values from 0 to 1
- tile_blocks: int32 [8, 8, 48, 2], P('row', 'rep'), may hold values from 0 to 7
- tile_count: int32 [8, 8], P('row', 'rep'), may hold values from 1 to 48, as said below
- cotangent: bfloat16 [8192, 256], P(('row', 'rep')), may hold values from -6 to 6
Outputs:
- output: bfloat16 [8192, 256], P(('row', 'rep'))
- grad_self: float32 [256, 256], replicated
- grad_neigh: float32 [256, 256], replicated
- grad_features: bfloat16 [8192, 256], P(('row', 'rep'))
Inputs may be any that keep to these rules, and one draw needn't show every extreme that they name: `tile_count`: for some row index and section all 48 slots are live in every draw.
All inputs are finite; a program needn't handle non-finite values.
Results may differ from a plain program's by a relative error of at most 0.024.
Values may be sent and summed in bfloat16 or wider, within the bound.
A program may use at most 64 MiB of HBM per device.

v0:
```python
import jax
import jax.numpy as jnp
from jax import lax
from jax.sharding import PartitionSpec as P


def from_root(value, axis, source):
    kept = jnp.where(lax.axis_index(axis) == source, value, 0).astype(value.dtype)
    return lax.psum(kept, axis)


def hot_tables(blocks, count, nblk, slots):
    live = (jnp.arange(slots) < count).astype(jnp.float32)
    dest_hot = (blocks[:, 0][:, None] == jnp.arange(nblk)[None, :]).astype(jnp.float32) * live[
        :, None
    ]
    src_hot = (blocks[:, 1][:, None] == jnp.arange(nblk)[None, :]).astype(jnp.float32)
    return (dest_hot, src_hot)


def body(
    features, weight_self, weight_neigh, degrees, tile_values, tile_blocks, tile_count, cotangent
):
    rows, width = features.shape
    tile = tile_values.shape[3]
    slots = tile_values.shape[2]
    sections_here = tile_values.shape[1]
    nblk = rows // tile
    nrep = lax.axis_size("rep")
    share = rows // nrep
    rep_pos = lax.axis_index("rep")
    row_pos = lax.axis_index("row")
    partial_value = jnp.zeros((nblk, tile, width), jnp.float32)
    for section in range(sections_here):
        source = from_root(features, "row", rep_pos * sections_here + section)
        source_blocks = source.reshape(nblk, tile, width)
        dest_hot, src_hot = hot_tables(tile_blocks[0, section], tile_count[0, section], nblk, slots)
        picked = jnp.einsum(
            "tc,cif->tif",
            src_hot.astype(jnp.bfloat16),
            source_blocks,
            preferred_element_type=jnp.bfloat16,
        )
        prod = jnp.einsum(
            "tij,tjf->tif", tile_values[0, section], picked, preferred_element_type=jnp.float32
        )
        partial_value = partial_value + jnp.einsum("tb,tif->bif", dest_hot, prod)
    partial_value = partial_value.reshape(rows, width)
    degree_all = degrees.astype(jnp.float32)[:, None]
    degree_mine = lax.dynamic_slice_in_dim(degree_all, rep_pos * share, share, 0)
    feat_mine = lax.dynamic_slice_in_dim(features, rep_pos * share, share, 0)
    agg_part = lax.psum_scatter(partial_value, "rep", scatter_dimension=0, tiled=True)
    agg_mine = (agg_part / degree_mine).astype(jnp.bfloat16)
    pre = jnp.dot(feat_mine, weight_self, preferred_element_type=jnp.float32) + jnp.dot(
        agg_mine, weight_neigh, preferred_element_type=jnp.float32
    )
    sig = jax.nn.sigmoid(pre)
    gpre_mine = (cotangent.astype(jnp.float32) * sig * (1.0 + pre * (1.0 - sig))).astype(
        jnp.bfloat16
    )
    dagg_mine = (
        jnp.dot(gpre_mine, weight_neigh.T, preferred_element_type=jnp.float32) / degree_mine
    ).astype(jnp.bfloat16)
    dagg_all = lax.all_gather(dagg_mine, "rep", axis=0, tiled=True)
    output = jax.nn.silu(pre).astype(jnp.bfloat16)
    grad_self_part = jnp.dot(feat_mine.T, gpre_mine, preferred_element_type=jnp.float32)
    grad_neigh_part = jnp.dot(agg_mine.T, gpre_mine, preferred_element_type=jnp.float32)
    grad_self, grad_neigh = lax.psum((grad_self_part, grad_neigh_part), ("row", "rep"))
    dagg_blocks = dagg_all.reshape(nblk, tile, width)
    terms = []
    for section in range(sections_here):
        dest_hot, src_hot = hot_tables(tile_blocks[0, section], tile_count[0, section], nblk, slots)
        picked = jnp.einsum(
            "tb,bif->tif",
            dest_hot.astype(jnp.bfloat16),
            dagg_blocks,
            preferred_element_type=jnp.bfloat16,
        )
        contrib = jnp.einsum(
            "tij,tif->tjf", tile_values[0, section], picked, preferred_element_type=jnp.float32
        )
        terms.append(jnp.einsum("tc,tjf->cjf", src_hot, contrib).reshape(rows, width))
    stacked = jnp.stack(terms, 0)
    summed = lax.psum(stacked, "row")
    owned = lax.dynamic_index_in_dim(summed, row_pos % sections_here, 0, keepdims=False).astype(
        jnp.bfloat16
    )
    everyone = from_root(owned, "rep", row_pos // sections_here)
    back_mine = lax.dynamic_slice_in_dim(everyone, rep_pos * share, share, 0)
    grad_features = (
        jnp.dot(gpre_mine, weight_self.T, preferred_element_type=jnp.float32)
        + back_mine.astype(jnp.float32)
    ).astype(jnp.bfloat16)
    return (output, grad_self, grad_neigh, grad_features)


def solution(mesh):
    in_specs = (
        P("row", None),
        P(),
        P(),
        P("row"),
        P("row", "rep", None, None, None),
        P("row", "rep", None, None),
        P("row", "rep"),
        P(("row", "rep"), None),
    )
    out_specs = (P(("row", "rep"), None), P(), P(), P(("row", "rep"), None))
    return jax.shard_map(body, mesh=mesh, in_specs=in_specs, out_specs=out_specs, check_vma=False)
```

profile of v0, /device:TPU:0, one launch (start us, length us, event | category | flops | bytes accessed | tf_op | source)
XLA Modules:
  0.0 399.4 jit_solution(14081113110862203722)
XLA Ops:
  7.2 2.3 broadcast_select_fusion.1
  13.0 57.8 %all-reduce.11.cloned.1.call-done = (bf16[8,128,256]{2,1,0:T(8,128)(2,1)}, bf16[8,128,256]{2,1,0:T(8,128)(2,1)}) async-done(((bf16[8,128,256]{2,1,0:T(8,128)(2,1)}, bf16[8,128,256]{2,1,0:T(8,128)(2,1)}), (bf16[8,128,256]{2,1,0:T(8,128)(2,1)}, bf16[8,128,256]{2,1,0:T(8,128)(2,1)})) %all-reduce.11.cloned.1.call-update) | async-done | bytes 1048592 | tf_op jit(solution)/shard_map/psum | solution.py:9
  70.7 2.1 fusion.31
  72.8 3.3 fusion.12
  76.0 3.8 copy.22
  79.9 2.2 fusion.33
  82.1 3.2 fusion.14
  85.3 4.9 %copy.19 = bf16[48,256,128]{1,0,2:T(8,128)(2,1)} copy(bf16[48,256,128]{2,1,0:T(8,128)(2,1)} %fusion.14) | data formatting | bytes 6291456 | tf_op jit(solution)/shard_map/tij,tjf->tif/dot_general | solution.py:44
  95.3 25.4 %reduce-scatter.2.cloned.1.call-done = f32[256,256]{1,0:T(8,128)} async-done(((f32[1024,256]{1,0:T(8,128)}), f32[256,256]{1,0:T(8,128)}) %reduce-scatter.2.cloned.1.call-update) | async-done | bytes 262160 | tf_op jit(solution)/shard_map/reduce_scatter | solution.py:52
  120.7 1.9 multiply_convert_fusion
  122.9 16.2 %all_gather.3 = bf16[1024,256]{1,0:T(8,128)(2,1)S(1)} all-gather(bf16[256,256]{1,0:T(8,128)(2,1)S(1)} %fusion.28), channel_id=1, replica_groups=mesh['row'=8,'rep'=4] {'rep'}, dimensions={0}, use_global_device_ids=true | all-gather | bytes 655360 | tf_op jit(solution)/shard_map/all_gather | solution.py:64
  140.1 2.7 fusion.35
  142.8 3.1 fusion.10
  145.9 3.8 copy.25
  153.0 3.1 fusion.8
  156.1 3.8 copy.27
  161.3 56.4 %all-reduce.12 = bf16[2,1024,256]{2,1,0:T(8,128)(2,1)S(1)} all-reduce(f32[2,1024,256]{2,1,0:T(8,128)S(1)} %pad_maximum_fusion), channel_id=1, replica_groups=mesh['row'=8,'rep'=4] {'row'}, use_global_device_ids=true, to_apply=%region_5.6 | all-reduce | flops 524288 | bytes 3145728 | tf_op jit(solution)/shard_map/psum | solution.py:84
  218.6 1.8 fusion.39
  220.4 2.0 fusion.77
  222.4 32.1 %all-reduce.7.cloned.1.call-done = bf16[1024,256]{1,0:T(8,128)(2,1)} async-done(((bf16[1024,256]{1,0:T(8,128)(2,1)}), bf16[1024,256]{1,0:T(8,128)(2,1)}) %all-reduce.7.cloned.1.call-update) | async-done | bytes 524304 | tf_op jit(solution)/shard_map/psum | solution.py:9
  254.5 1.8 fusion.27
  256.3 133.3 %all-reduce.9.cloned.1.call-done = (f32[256,256]{1,0:T(8,128)}, f32[256,256]{1,0:T(8,128)}) async-done(((f32[256,256]{1,0:T(8,128)}, f32[256,256]{1,0:T(8,128)}), (f32[256,256]{1,0:T(8,128)}, f32[256,256]{1,0:T(8,128)})) %all-reduce.9.cloned.1.call-update) | async-done | bytes 524304 | tf_op jit(solution)/shard_map/psum | solution.py:68
  389.6 1.7 copy.51
  391.2 1.7 copy.52
  (61 shorter events, 15.1 us)
Async XLA Ops:
  7.2 113.6 %copy-start = (bf16[256,256]{1,0:T(8,128)(2,1)S(1)}, bf16[256,256]{1,0:T(8,128)(2,1)}, u32[]{:S(2)}) copy-start(bf16[256,256]{1,0:T(8,128)(2,1)} %param.10) | copy-start | bytes 393220
  7.2 63.5 %all-reduce.11.cloned.1.call-start = ((), (), s32[]{:S(2)}) async-start(), calls=%async_computation.4 | async-start | bytes 2097152 | tf_op jit(solution)/shard_map/psum | solution.py:9
  7.2 65.5 %copy-start.3 = (bf16[1,2,48,128,128]{4,3,2,1,0:T(8,128)(2,1)S(1)}, bf16[1,2,48,128,128]{4,3,2,1,0:T(8,128)(2,1)}, u32[]{:S(2)}) copy-start(bf16[1,2,48,128,128]{4,3,2,1,0:T(8,128)(2,1)} %param.12) | copy-start | bytes 9437188
  9.5 111.2 %reduce-scatter.2.cloned.1.call-start = ((), (), s32[]{:S(2)}) async-start(), calls=%async_computation.1 | async-start | bytes 1310720 | tf_op jit(solution)/shard_map/reduce_scatter | solution.py:52
  11.6 78.7 %copy-start.10 = (bf16[48]{0:T(256)(128)(2,1)}, bf16[48]{0:T(256)(128)(2,1)S(1)}, u32[]{:S(2)}) copy-start(bf16[48]{0:T(256)(128)(2,1)S(1)} %compare_convert_fusion) | copy-start | bytes 292
  12.2 78.5 %copy-start.12 = (bf16[48]{0:T(256)(128)(2,1)}, bf16[48]{0:T(256)(128)(2,1)S(1)}, u32[]{:S(2)}) copy-start(bf16[48]{0:T(256)(128)(2,1)S(1)} %compare_convert_fusion.1) | copy-start | bytes 292
  79.9 2.2 copy-start.4
  90.2 1.9 copy-start.1
  92.1 1.9 copy-start.9
  92.1 2.1 copy-start.8
  92.7 28.1 %copy-start.16 = (bf16[256,256]{1,0:T(8,128)(2,1)S(1)}, bf16[256,256]{1,0:T(8,128)(2,1)}, u32[]{:S(2)}) copy-start(bf16[256,256]{1,0:T(8,128)(2,1)} %param.15) | copy-start | bytes 393220
  94.0 45.1 %copy-start.13 = (bf16[48]{0:T(256)(128)(2,1)S(1)}, bf16[48]{0:T(256)(128)(2,1)}, u32[]{:S(2)}) copy-start(bf16[48]{0:T(256)(128)(2,1)} %copy-done.12) | copy-start | bytes 292
  94.0 160.5 %all-reduce.7.cloned.1.call-start = ((), (), s32[]{:S(2)}) async-start(), calls=%async_computation.2 | async-start | bytes 1048576 | tf_op jit(solution)/shard_map/psum | solution.py:9
  94.2 45.9 %copy-start.14 = (f32[256]{0:T(256)}, f32[256]{0:T(256)S(1)}, u32[]{:S(2)}) copy-start(f32[256]{0:T(256)S(1)} %dynamic-slice.3) | copy-start | bytes 3076
  122.7 17.5 %copy-start.11 = (bf16[48]{0:T(256)(128)(2,1)S(1)}, bf16[48]{0:T(256)(128)(2,1)}, u32[]{:S(2)}) copy-start(bf16[48]{0:T(256)(128)(2,1)} %copy-done.10) | copy-start | bytes 292
  139.1 3.7 copy-start.5
  149.8 2.1 copy-start.2
  149.8 3.2 copy-start.6
  159.9 1.2 copy-start.7
  161.3 59.1 %copy-start.15 = (f32[256]{0:T(256)S(1)}, f32[256]{0:T(256)}, u32[]{:S(2)}) copy-start(f32[256]{0:T(256)} %copy-done.14) | copy-start | bytes 3076
  218.5 171.0 %all-reduce.9.cloned.1.call-start = ((), (), s32[]{:S(2)}) async-start(), calls=%async_computation.3 | async-start | bytes 1048576 | tf_op jit(solution)/shard_map/psum | solution.py:68
Sparse Core Ops, SparseCore 0:
  11.2 59.4 all-reduce.10
  94.1 26.5 reduce-scatter.1
  218.7 35.8 all-reduce.6
  260.4 129.1 all-reduce.8
where the time goes:
time: 400 us; the launch traced here: 399 us
  waiting for transfers between devices  249 us (62%)
  blocking collectives  72.6 us (18%)
  matrix products  31.5 us (8%)
  local copies, waits for them, and re-layouts  28 us (7%)
  between operations  14 us (4%)
  other arithmetic  4.54 us (1%)
    psum x1, waiting for transfers between devices, body(): lax.psum((grad_self_part, grad_neigh_part), ('row', 'rep'))  133 us
    psum x2, waiting for transfers between devices, from_root(): return lax.psum(kept, axis)  89.8 us
    psum x1, blocking collectives, body(): summed = lax.psum(stacked, 'row')  56.4 us
    reduce_scatter x1, waiting for transfers between devices, body(): lax.psum_scatter(partial_value, 'rep', scatter_dimension=0, tiled=True)  25.4 us
    all_gather x1, blocking collectives, body(): dagg_all = lax.all_gather(dagg_mine, 'rep', axis=0, tiled=True)  16.2 us
    dot_general x2, local copies, waits for them, and re-layouts, body(): jnp.einsum('tij,tjf->tif', tile_values[0, section], picked, preferred_ele...  8.77 us
  transfers between devices with their start and end apart: 4, of which 4 were waited for; matrix products, arithmetic and copies ran while one was open for 3% of the time, Pallas kernels for 0%

commit v1 on v0

--- a/solution.py
+++ b/solution.py
@@ -65,7 +65,7 @@
     output = jax.nn.silu(pre).astype(jnp.bfloat16)
     grad_self_part = jnp.dot(feat_mine.T, gpre_mine, preferred_element_type=jnp.float32)
     grad_neigh_part = jnp.dot(agg_mine.T, gpre_mine, preferred_element_type=jnp.float32)
-    grad_self, grad_neigh = lax.psum((grad_self_part, grad_neigh_part), ("row", "rep"))
+    grad_self, grad_neigh = lax.psum(lax.psum((grad_self_part, grad_neigh_part), "rep"), "row")
     dagg_blocks = dagg_all.reshape(nblk, tile, width)
     terms = []
     for section in range(sections_here):

time: 400 us -> 326 us (0.81)
  waiting for transfers between devices: 249 us -> 176 us
    psum x1 -> x2, waiting for transfers between devices: 133 us -> 55.9 us  [the longest x1 55.9 us: body(): lax.psum(lax.psum((grad_self_part, grad_neigh_part), 'rep'), 'row')]
  transfers between devices with their start and end apart: 4 -> 5, of which waited for: 4 -> 4; matrix products, arithmetic and copies ran while one was open for 3% -> 2% of each run, Pallas kernels for 0% -> 0%
where the time goes in v1:
time: 326 us; the launch traced here: 325 us
  waiting for transfers between devices  176 us (54%)
  blocking collectives  73.4 us (23%)
  matrix products  28.7 us (9%)
  local copies, waits for them, and re-layouts  28.3 us (9%)
  between operations  14.1 us (4%)
  other arithmetic  4.58 us (1%)
    psum x2, waiting for transfers between devices, from_root(): return lax.psum(kept, axis)  93 us
    psum x1, blocking collectives, body(): summed = lax.psum(stacked, 'row')  57.3 us
    psum x1, waiting for transfers between devices, body(): lax.psum(lax.psum((grad_self_part, grad_neigh_part), 'rep'), 'row')  55.9 us
    reduce_scatter x1, waiting for transfers between devices, body(): lax.psum_scatter(partial_value, 'rep', scatter_dimension=0, tiled=True)  26.3 us
    all_gather x1, blocking collectives, body(): dagg_all = lax.all_gather(dagg_mine, 'rep', axis=0, tiled=True)  16.2 us
    dot_general x2, local copies, waits for them, and re-layouts, body(): jnp.einsum('tij,tjf->tif', tile_values[0, section], picked, preferred_ele...  8.8 us
    dot_general x2, local copies, waits for them, and re-layouts, body(): jnp.einsum('tij,tif->tjf', tile_values[0, section], picked, preferred_ele...  7.7 us
    unnamed x40, local copies, waits for them, and re-layouts  6.74 us
  transfers between devices with their start and end apart: 5, of which 4 were waited for; matrix products, arithmetic and copies ran while one was open for 2% of the time, Pallas kernels for 0%

profile of v1, /device:TPU:0, one launch (start us, length us, event | category | flops | bytes accessed | tf_op | source)
XLA Modules:
  0.0 325.1 jit_solution(15807273443050486945)
XLA Ops:
  7.2 2.3 broadcast_select_fusion.1
  13.0 57.7 %all-reduce.15.cloned.1.call-done = (bf16[8,128,256]{2,1,0:T(8,128)(2,1)}, bf16[8,128,256]{2,1,0:T(8,128)(2,1)}) async-done(((bf16[8,128,256]{2,1,0:T(8,128)(2,1)}, bf16[8,128,256]{2,1,0:T(8,128)(2,1)}), (bf16[8,128,256]{2,1,0:T(8,128)(2,1)}, bf16[8,128,256]{2,1,0:T(8,128)(2,1)})) %all-reduce.15.cloned.1.call-update) | async-done | bytes 1048592 | tf_op jit(solution)/shard_map/psum | solution.py:9
  70.7 2.1 fusion.31
  72.8 3.2 fusion.12
  76.0 3.8 %copy.22 = bf16[48,256,128]{1,0,2:T(8,128)(2,1)S(1)} copy(bf16[48,256,128]{2,1,0:T(8,128)(2,1)} %fusion.12) | data formatting | bytes 6291456 | tf_op jit(solution)/shard_map/tij,tjf->tif/dot_general | solution.py:44
  79.9 2.2 fusion.33
  82.1 3.2 fusion.14
  85.3 5.0 %copy.19 = bf16[48,256,128]{1,0,2:T(8,128)(2,1)} copy(bf16[48,256,128]{2,1,0:T(8,128)(2,1)} %fusion.14) | data formatting | bytes 6291456 | tf_op jit(solution)/shard_map/tij,tjf->tif/dot_general | solution.py:44
  90.8 1.4 copy-done.1
  92.7 1.3 copy.14
  94.4 26.3 %reduce-scatter.2.cloned.1.call-done = f32[256,256]{1,0:T(8,128)} async-done(((f32[1024,256]{1,0:T(8,128)}), f32[256,256]{1,0:T(8,128)}) %reduce-scatter.2.cloned.1.call-update) | async-done | bytes 262160 | tf_op jit(solution)/shard_map/reduce_scatter | solution.py:52
  120.8 1.9 multiply_convert_fusion
  122.9 16.2 %all_gather.3 = bf16[1024,256]{1,0:T(8,128)(2,1)S(1)} all-gather(bf16[256,256]{1,0:T(8,128)(2,1)S(1)} %fusion.28), channel_id=1, replica_groups=mesh['row'=8,'rep'=4] {'rep'}, dimensions={0}, use_global_device_ids=true | all-gather | bytes 655360 | tf_op jit(solution)/shard_map/all_gather | solution.py:64
  140.2 2.6 fusion.35
  143.7 3.1 fusion.10
  146.8 3.8 %copy.25 = bf16[48,256,128]{1,0,2:T(8,128)(2,1)S(1)} copy(bf16[48,256,128]{2,1,0:T(8,128)(2,1)} %fusion.10) | data formatting | bytes 6291456 | tf_op jit(solution)/shard_map/tij,tif->tjf/dot_general | solution.py:79
  153.9 3.1 fusion.8
  157.0 3.8 %copy.27 = bf16[48,256,128]{1,0,2:T(8,128)(2,1)S(1)} copy(bf16[48,256,128]{2,1,0:T(8,128)(2,1)} %fusion.8) | data formatting | bytes 6291456 | tf_op jit(solution)/shard_map/tij,tif->tjf/dot_general | solution.py:79
  163.5 57.3 %all-reduce.16 = bf16[2,1024,256]{2,1,0:T(8,128)(2,1)S(1)} all-reduce(f32[2,1024,256]{2,1,0:T(8,128)S(1)} %pad_maximum_fusion), channel_id=1, replica_groups=mesh['row'=8,'rep'=4] {'row'}, use_global_device_ids=true, to_apply=%region_7.8 | all-reduce | flops 524288 | bytes 3145728 | tf_op jit(solution)/shard_map/psum | solution.py:84
  222.3 35.3 %all-reduce.9.cloned.1.call-done = bf16[1024,256]{1,0:T(8,128)(2,1)} async-done(((bf16[1024,256]{1,0:T(8,128)(2,1)}), bf16[1024,256]{1,0:T(8,128)(2,1)}) %all-reduce.9.cloned.1.call-update) | async-done | bytes 524304 | tf_op jit(solution)/shard_map/psum | solution.py:9
  257.5 1.8 fusion.27
  259.3 55.9 %all-reduce.11.cloned.1.call-done = (f32[256,256]{1,0:T(8,128)}, f32[256,256]{1,0:T(8,128)}) async-done(((f32[256,256]{1,0:T(8,128)}, f32[256,256]{1,0:T(8,128)}), (f32[256,256]{1,0:T(8,128)}, f32[256,256]{1,0:T(8,128)})) %all-reduce.11.cloned.1.call-update) | async-done | bytes 524304 | tf_op jit(solution)/shard_map/psum | solution.py:68
  315.2 1.7 copy.53
  316.9 1.7 copy.54
  (68 shorter events, 14.3 us)
Async XLA Ops:
  7.2 113.6 %copy-start = (bf16[256,256]{1,0:T(8,128)(2,1)S(1)}, bf16[256,256]{1,0:T(8,128)(2,1)}, u32[]{:S(2)}) copy-start(bf16[256,256]{1,0:T(8,128)(2,1)} %param.10) | copy-start | bytes 393220
  7.2 63.5 %all-reduce.15.cloned.1.call-start = ((), (), s32[]{:S(2)}) async-start(), calls=%async_computation.5 | async-start | bytes 2097152 | tf_op jit(solution)/shard_map/psum | solution.py:9
  7.2 65.5 %copy-start.3 = (bf16[1,2,48,128,128]{4,3,2,1,0:T(8,128)(2,1)S(1)}, bf16[1,2,48,128,128]{4,3,2,1,0:T(8,128)(2,1)}, u32[]{:S(2)}) copy-start(bf16[1,2,48,128,128]{4,3,2,1,0:T(8,128)(2,1)} %param.12) | copy-start | bytes 9437188
  9.6 111.2 %reduce-scatter.2.cloned.1.call-start = ((), (), s32[]{:S(2)}) async-start(), calls=%async_computation.1 | async-start | bytes 1310720 | tf_op jit(solution)/shard_map/reduce_scatter | solution.py:52
  11.6 78.7 %copy-start.11 = (bf16[48]{0:T(256)(128)(2,1)}, bf16[48]{0:T(256)(128)(2,1)S(1)}, u32[]{:S(2)}) copy-start(bf16[48]{0:T(256)(128)(2,1)S(1)} %compare_convert_fusion) | copy-start | bytes 292
  12.2 78.5 %copy-start.13 = (bf16[48]{0:T(256)(128)(2,1)}, bf16[48]{0:T(256)(128)(2,1)S(1)}, u32[]{:S(2)}) copy-start(bf16[48]{0:T(256)(128)(2,1)S(1)} %compare_convert_fusion.1) | copy-start | bytes 292
  79.9 2.2 copy-start.4
  90.3 1.9 copy-start.1
  92.1 2.0 copy-start.10
  92.2 2.1 copy-start.8
  92.2 2.1 copy-start.9
  92.7 28.1 %copy-start.18 = (bf16[256,256]{1,0:T(8,128)(2,1)S(1)}, bf16[256,256]{1,0:T(8,128)(2,1)}, u32[]{:S(2)}) copy-start(bf16[256,256]{1,0:T(8,128)(2,1)} %param.15) | copy-start | bytes 393220
  94.0 45.1 %copy-start.14 = (bf16[48]{0:T(256)(128)(2,1)S(1)}, bf16[48]{0:T(256)(128)(2,1)}, u32[]{:S(2)}) copy-start(bf16[48]{0:T(256)(128)(2,1)} %copy-done.13) | copy-start | bytes 292
  94.0 127.7 %all-reduce.13.cloned.1.call-start = ((), (), s32[]{:S(2)}) async-start(), calls=%async_computation.4 | async-start | bytes 1048576 | tf_op jit(solution)/shard_map/psum | solution.py:68
  94.2 45.9 %copy-start.15 = (f32[256]{0:T(256)}, f32[256]{0:T(256)S(1)}, u32[]{:S(2)}) copy-start(f32[256]{0:T(256)S(1)} %dynamic-slice.3) | copy-start | bytes 3076
  122.7 17.4 %copy-start.12 = (bf16[48]{0:T(256)(128)(2,1)S(1)}, bf16[48]{0:T(256)(128)(2,1)}, u32[]{:S(2)}) copy-start(bf16[48]{0:T(256)(128)(2,1)} %copy-done.11) | copy-start | bytes 292
  139.1 4.6 %copy-start.5 = (bf16[1,2,48,128,128]{4,3,2,1,0:T(8,128)(2,1)S(1)}, bf16[1,2,48,128,128]{4,3,2,1,0:T(8,128)(2,1)}, u32[]{:S(2)}) copy-start(bf16[1,2,48,128,128]{4,3,2,1,0:T(8,128)(2,1)} %param.12) | copy-start | bytes 9437188
  150.7 2.1 copy-start.2
  150.7 3.2 copy-start.6
  160.9 1.2 copy-start.7
  161.4 0.8 copy-start.16
  161.4 1.0 copy-start.17
  163.5 94.1 %all-reduce.9.cloned.1.call-start = ((), (), s32[]{:S(2)}) async-start(), calls=%async_computation.2 | async-start | bytes 1048576 | tf_op jit(solution)/shard_map/psum | solution.py:9
  221.7 93.6 %all-reduce.11.cloned.1.call-start = ((), (), s32[]{:S(2)}) async-start(), calls=%async_computation.3 | async-start | bytes 1048576 | tf_op jit(solution)/shard_map/psum | solution.py:68
Sparse Core Ops, SparseCore 0:
  11.2 59.4 all-reduce.14
  94.2 26.5 reduce-scatter.1
  163.6 36.9 all-reduce.12
  221.8 35.7 all-reduce.8
  260.5 54.6 all-reduce.10
